TPU v7x, 32 devices: a whole 2x2x4 slice. The times are simulated.
32 devices in a mesh: grp: 4 (over y, core), leaf: 8 (over z, x).
Axes of the slice: x: 2, y: 2, z: 4, core: 2. Of those that a mesh axis runs over, the one named last changes fastest.
Arguments:
- points: bfloat16 [131072, 64], P(('grp', 'leaf')), may hold values from -6 to 6
- solution: float32 [131072, 64], P(('grp', 'leaf')), may hold values from -6 to 6
- residual: float32 [131072, 64], P(('grp', 'leaf')), may hold values from -150 to 150
- direction: float32 [131072, 64], P(('grp', 'leaf')), may hold values from -150 to 150
- near: int32 [128, 3], P(('grp', 'leaf')), may hold values from -1 to 127, as said below
- bases: bfloat16 [128, 1024, 256], P(('grp', 'leaf')), may hold values from -0.1875 to 0.1875
- leaf_transfer: bfloat16 [128, 256, 256], P(('grp', 'leaf')), may hold values from -0.1875 to 0.1875
- inner_transfer: bfloat16 [3, 2, 256, 256], replicated, may hold values from -1 to 1
- inner_coupling: bfloat16 [3, 256, 256], replicated, may hold values from -1 to 1
- outer_transfer: bfloat16 [2, 2, 256, 256], replicated, may hold values from -1 to 1
- outer_coupling: bfloat16 [2, 256, 256], replicated, may hold values from -1 to 1
Outputs:
- new_solution: float32 [131072, 64], P(('grp', 'leaf'))
- new_residual: float32 [131072, 64], P(('grp', 'leaf'))
- new_direction: float32 [131072, 64], P(('grp', 'leaf'))
Inputs may be any that keep to these rules, and one draw needn't show every extreme that they name: Row i of near is (i, i - 1 or -1, i + 1 or -1); leaf i lists i + 1 exactly when leaf i + 1 lists i; the last leaf of each aligned block of 4 leaves lists the next leaf whenever there is one.
All inputs are finite; a program needn't handle non-finite values.
Results may differ from a plain program's by a relative error of at most 0.0027.
Values may be sent and summed in bfloat16 or wider, within the bound.
A program may use at most 128 MiB of HBM per device.

v0:
```python
import jax
import jax.numpy as jnp
from jax import lax
from jax.sharding import PartitionSpec as P

highest = lax.Precision.HIGHEST
ridge = 2.0


def padded(cells, sides, width):
    for axis, dim in sides:
        count = lax.axis_size(axis)
        ends = count - 1
        head = lax.slice_in_dim(cells, 0, width, axis=dim)
        tail = lax.slice_in_dim(cells, cells.shape[dim] - width, cells.shape[dim], axis=dim)
        cells = jnp.concatenate(
            [
                lax.ppermute(tail, axis, [(i, (i + 1) % count) for i in range(ends)]),
                cells,
                lax.ppermute(head, axis, [((i + 1) % count, i) for i in range(ends)]),
            ],
            axis=dim,
        )
    return cells


def swapped(value, axis, stride):
    return lax.ppermute(value, axis, [(i, i ^ 1 << stride) for i in range(lax.axis_size(axis))])


def kernel_block(own, window, mask):
    own_wide = own.astype(jnp.float32)
    win_wide = window.astype(jnp.float32)
    sq_own = jnp.sum(own_wide * own_wide, axis=1)
    sq_win = jnp.sum(win_wide * win_wide, axis=1)
    cross = jnp.dot(own, window.T, preferred_element_type=jnp.float32)
    dist = sq_own[:, None] + sq_win[None, :] - 2.0 * cross
    return (jnp.exp(-dist * (2.0 / own.shape[1])) * mask[None, :]).astype(jnp.bfloat16)


def couple(other, side, q_level, b_level):
    left_first = side == 0
    q_mine = jnp.where(left_first, q_level[0], q_level[1])
    coupling_mat = jnp.where(left_first, b_level, b_level.T)
    return (q_mine, jnp.dot(coupling_mat, other, precision=highest))


def join_pair(own, other, side, q_level):
    left_first = side == 0
    q_mine = jnp.where(left_first, q_level[0], q_level[1])
    q_other = jnp.where(left_first, q_level[1], q_level[0])
    return jnp.dot(q_mine.T, own, precision=highest) + jnp.dot(q_other.T, other, precision=highest)


def flag_of(value):
    return jnp.where(value >= 0, 1.0, 0.0).astype(jnp.float32)


def body(
    points,
    solution,
    residual,
    direction,
    near,
    bases,
    leaf_transfer,
    inner_transfer,
    inner_coupling,
    outer_transfer,
    outer_coupling,
):
    leaf_dev = near.shape[0]
    leaf = bases.shape[1]
    dim = points.shape[1]
    nrhs = direction.shape[1]
    packed = direction.astype(jnp.bfloat16)
    joined = jnp.concatenate([points, packed], axis=1)
    extended = padded(joined, ((("grp", "leaf"), 0),), leaf)
    vectors = packed.reshape(leaf_dev, leaf, nrhs)
    skel = jnp.einsum("lpr,lpc->lrc", bases, vectors, preferred_element_type=jnp.float32)
    trans = leaf_transfer.astype(jnp.float32)
    node = jnp.einsum("lba,lbc->ac", trans, skel, precision=highest)
    inner_q = inner_transfer.astype(jnp.float32)
    inner_b = inner_coupling.astype(jnp.float32)
    outer_q = outer_transfer.astype(jnp.float32)
    outer_b = outer_coupling.astype(jnp.float32)
    records = []
    for level in range(inner_q.shape[0]):
        other = swapped(node, "leaf", level)
        side = lax.axis_index("leaf") >> level & 1
        records.append(couple(other, side, inner_q[level], inner_b[level]))
        node = join_pair(node, other, side, inner_q[level])
    for level in range(outer_q.shape[0]):
        other = swapped(node, "grp", level)
        side = lax.axis_index("grp") >> level & 1
        records.append(couple(other, side, outer_q[level], outer_b[level]))
        node = join_pair(node, other, side, outer_q[level])
    outputs = []
    for local in range(leaf_dev):
        window = extended[local * leaf : (local + 3) * leaf]
        own = points[local * leaf : (local + 1) * leaf]
        flags = near[local]
        blocks = jnp.stack([flag_of(flags[1]), jnp.ones((), jnp.float32), flag_of(flags[2])])
        mask = jnp.repeat(blocks, leaf)
        kern = kernel_block(own, window[:, :dim], mask)
        outputs.append(jnp.dot(kern, window[:, dim:], preferred_element_type=jnp.float32))
    near_term = jnp.concatenate(outputs, axis=0)
    incoming = jnp.zeros((node.shape[0], nrhs), jnp.float32)
    for q_mine, mine in reversed(records):
        incoming = mine + jnp.dot(q_mine, incoming, precision=highest)
    leaf_in = jnp.einsum("lab,bc->lac", trans, incoming, precision=highest).astype(jnp.bfloat16)
    far_term = jnp.einsum(
        "lpr,lrc->lpc", bases, leaf_in, preferred_element_type=jnp.float32
    ).reshape(-1, nrhs)
    image = ridge * direction + near_term + far_term
    rr, pq, rq, qq = lax.psum(
        (
            jnp.sum(residual * residual, axis=0),
            jnp.sum(direction * image, axis=0),
            jnp.sum(residual * image, axis=0),
            jnp.sum(image * image, axis=0),
        ),
        ("grp", "leaf"),
    )
    alpha = rr / pq
    new_solution = solution + alpha * direction
    new_residual = residual - alpha * image
    fresh = rr - 2.0 * alpha * rq + alpha * alpha * qq
    new_direction = new_residual + fresh / rr * direction
    return (new_solution, new_residual, new_direction)


def solution(mesh):
    in_specs = (
        P(("grp", "leaf"), None),
        P(("grp", "leaf"), None),
        P(("grp", "leaf"), None),
        P(("grp", "leaf"), None),
        P(("grp", "leaf"), None),
        P(("grp", "leaf"), None, None),
        P(("grp", "leaf"), None, None),
        P(),
        P(),
        P(),
        P(),
    )
    out_specs = (P(("grp", "leaf"), None), P(("grp", "leaf"), None), P(("grp", "leaf"), None))
    return jax.shard_map(body, mesh=mesh, in_specs=in_specs, out_specs=out_specs, check_vma=False)
```

profile of v0, /device:TPU:0, one launch (start us, length us, event | category | flops | bytes accessed | tf_op | source)
XLA Modules:
  0.0 146.2 jit_solution(7510675981744808651)
XLA Ops:
  0.7 1.4 convert_element_type.59
  3.0 1.0 fusion.103
  4.0 3.0 %collective-permute-start.2 = (f32[256,64]{0,1:T(8,128)}, f32[256,64]{0,1:T(8,128)}, u32[]{:S(2)}, u32[]{:S(2)}) collective-permute-start(f32[256,64]{0,1:T(8,128)} %bitcast.13), channel_id=1, source_target_pairs={{0,1},{1,0},{2,3},{3,2},{4,5},{5,4},{6,7},{7,6},{8,9},{9,8},{10,11... | collective-permute-start | bytes 196616 | tf_op jit(solution)/shard_map/ppermute | solution.py:28
  7.0 0.8 pad_maximum_fusion.14
  7.8 2.6 %collective-permute-start = (bf16[1024,128]{0,1:T(8,128)(2,1)}, bf16[1024,128]{0,1:T(8,128)(2,1)}, u32[]{:S(2)}, u32[]{:S(2)}) collective-permute-start(bf16[1024,128]{0,1:T(8,128)(2,1)} %get-tuple-element.26), channel_id=1, source_target_pairs={{0,1},{1,2},{2,3},{3,4},{4,5},{5,6},{6,7},{7,8},{8,9},{9,10},{10,1... | collective-permute-start | bytes 786440 | tf_op jit(solution)/shard_map/ppermute | solution.py:18
  10.4 1.3 collective-permute-start.1
  11.7 0.7 multiply_reduce_fusion.11
  12.5 2.5 %convert_element_type.72 = f32[3,2,256,256]{3,2,1,0:T(8,128)} convert(bf16[3,2,256,256]{3,2,1,0:T(8,128)(2,1)} %param.18) | non-fusion elementwise | flops 393216 | bytes 2359296 | tf_op jit(solution)/shard_map/convert_element_type | solution.py:83
  14.9 2.1 %convert_element_type.74 = f32[2,2,256,256]{3,2,1,0:T(8,128)} convert(bf16[2,2,256,256]{3,2,1,0:T(8,128)(2,1)} %param.20) | non-fusion elementwise | flops 262144 | bytes 1572864 | tf_op jit(solution)/shard_map/convert_element_type | solution.py:85
  17.1 0.8 copy-done.6
  17.9 0.7 slice_bitcast_fusion.1
  18.6 1.8 %copy.18 = f32[256,256]{0,1:T(8,128)} copy(f32[256,256]{1,0:T(8,128)} %get-tuple-element.31) | data formatting | bytes 524288 | tf_op jit(solution)/shard_map/squeeze | solution.py:96
  20.4 0.8 copy.17
  21.2 1.1 convert_element_type.71
  22.3 0.9 copy-done.4
  23.2 0.9 slice_bitcast_fusion.4
  24.0 1.8 %copy.16 = f32[256,256]{0,1:T(8,128)} copy(f32[256,256]{1,0:T(8,128)} %get-tuple-element.28) | data formatting | bytes 524288 | tf_op jit(solution)/shard_map/squeeze | solution.py:91
  25.8 0.8 copy.15
  26.7 1.1 copy.14
  34.6 1.9 %fusion.50 = f32[256,64]{0,1:T(8,128)} fusion(f32[3,2,256,256]{3,2,1,0:T(8,128)} %convert_element_type.72, pred[]{:T(512)S(6)} %eq.19, f32[64,256,1]{1,0,2:T(8,128)} %fusion.103), kind=kOutput, calls=%fused_computation.92 | convolution fusion | flops 50397184 | bytes 655361 | tf_op jit(solution)/shard_map/dot_general | solution.py:52
  36.6 1.4 fusion.29
  39.3 0.7 broadcast_in_dim.11
  40.6 0.7 broadcast_in_dim.12
  41.9 1.4 convolution_add_fusion.8
  43.3 4.5 %collective-permute-start.3 = (f32[256,64]{0,1:T(8,128)S(1)}, f32[256,64]{0,1:T(8,128)S(1)}, u32[]{:S(2)}, u32[]{:S(2)}) collective-permute-start(f32[256,64]{0,1:T(8,128)S(1)} %convolution_add_fusion.8), channel_id=1, source_target_pairs={{0,2},{1,3},{2,0},{3,1},{4,6},{5,7},{6,4},{7,5},{8,10},{9,11},{10,... | collective-permute-start | bytes 196616 | tf_op jit(solution)/shard_map/ppermute | solution.py:28
  47.8 1.3 fusion.45
  49.1 1.1 collective-permute-done.3
  50.2 1.3 convolution_add_fusion.7
  51.5 2.9 %collective-permute-start.4 = (f32[256,64]{0,1:T(8,128)S(1)}, f32[256,64]{0,1:T(8,128)S(1)}, u32[]{:S(2)}, u32[]{:S(2)}) collective-permute-start(f32[256,64]{0,1:T(8,128)S(1)} %convolution_add_fusion.7), channel_id=1, source_target_pairs={{0,4},{1,5},{2,6},{3,7},{4,0},{5,1},{6,2},{7,3},{8,12},{9,13},{10,... | collective-permute-start | bytes 196616 | tf_op jit(solution)/shard_map/ppermute | solution.py:28
  54.5 1.3 fusion.40
  55.8 1.3 collective-permute-done.4
  57.1 1.3 convolution_add_fusion.6
  59.8 1.2 convolution_add_fusion.1
  61.1 4.0 %collective-permute-start.6 = (f32[256,64]{1,0:T(8,128)}, f32[256,64]{1,0:T(8,128)}, u32[]{:S(2)}, u32[]{:S(2)}) collective-permute-start(f32[256,64]{1,0:T(8,128)} %convolution_add_fusion.1), channel_id=1, source_target_pairs={{0,16},{8,24},{16,0},{24,8},{1,17},{9,25},{17,1},{25,9},{2,18},{10... | collective-permute-start | bytes 196616 | tf_op jit(solution)/shard_map/ppermute | solution.py:28
  65.1 2.0 %multiply_reduce_fusion.7 = (f32[3072]{0:T(1024)}, f32[3072]{0:T(1024)}, f32[3072]{0:T(1024)}, f32[3072]{0:T(1024)S(1)}) fusion(bf16[4096,64]{0,1:T(8,128)(2,1)S(1)} %convert_element_type.59, bf16[4096,64]{0,1:T(8,128)(2,1)S(1)} %copy-done.1, bf16[1024,128]{0,1:T(8,128)(2,1)} %collective-permute-done, bf16[1024,128]{0,1:T(8,128)(2,1)} %collective-permute-done.1), kind=kLoop, calls=%fused_computation.43 | loop fusion | flops 4313088 | bytes 2408448 | tf_op jit(solution)/shard_map/reduce_sum | solution.py:35
  67.0 6.0 %fusion.10 = f32[1024,64]{0,1:T(8,128)} fusion(f32[3072]{0:T(1024)} %mul.164, f32[3072]{0:T(1024)} %get-tuple-element.13, f32[1024]{0:T(1024)} %get-tuple-element.11, bf16[4096,64]{0,1:T(8,128)(2,1)S(1)} %convert_element_type.59, bf16[4096,64]{0,1:T(8,128)(2,1)S(1)} %copy-done.1), kind=kOutput, calls=%fused_computation.14 | convolution fusion | flops 827326464 | bytes 1208320 | tf_op jit(solution)/shard_map/dot_general | solution.py:106
  73.0 6.5 %fusion.12 = f32[1024,64]{0,1:T(8,128)} fusion(f32[3072]{0:T(1024)} %mul.157, f32[3072]{0:T(1024)} %get-tuple-element.7, f32[1024]{0:T(1024)S(1)} %copy-done.24, bf16[1024,128]{0,1:T(8,128)(2,1)} %collective-permute-done, bf16[4096,64]{0,1:T(8,128)(2,1)S(1)} %convert_element_type.59, bf16[4096,64]{0,1:T(8,128)(2,1)S(1)} %copy-done.1), kind=kOutput, calls=%fused_computation.16 | convolution fusion | flops 829685760 | bytes 3043328 | tf_op jit(solution)/shard_map/dot_general | solution.py:106
  79.6 6.4 %fusion.13 = f32[1024,64]{0,1:T(8,128)} fusion(f32[3072]{0:T(1024)} %mul.179, f32[3072]{0:T(1024)} %get-tuple-element.8, f32[1024]{0:T(1024)} %get-tuple-element.12, bf16[1024,128]{0,1:T(8,128)(2,1)} %collective-permute-done.1, bf16[4096,64]{0,1:T(8,128)(2,1)S(1)} %convert_element_type.59, bf16[4096,64]{0,1:T(8,128)(2,1)S(1)} %copy-done.1), kind=kOutput, calls=%fused_computation.17 | convolution fusion | flops 829685760 | bytes 3043328 | tf_op jit(solution)/shard_map/dot_general | solution.py:106
  86.0 6.0 %fusion.11 = f32[1024,64]{0,1:T(8,128)} fusion(f32[3072]{0:T(1024)} %mul.171, f32[3072]{0:T(1024)S(1)} %get-tuple-element.14, f32[1024]{0:T(1024)S(1)} %copy-done.23, bf16[4096,64]{0,1:T(8,128)(2,1)S(1)} %convert_element_type.59, bf16[4096,64]{0,1:T(8,128)(2,1)S(1)} %copy-done.1), kind=kOutput, calls=%fused_computation.15 | convolution fusion | flops 827326464 | bytes 1208320 | tf_op jit(solution)/shard_map/dot_general | solution.py:106
  92.0 1.6 %convolution_add_fusion = f32[256,64]{1,0:T(8,128)S(1)} fusion(f32[256,64]{1,0:T(8,128)S(1)} %fusion.29, f32[256,64]{1,0:T(8,128)} %collective-permute-done.6, f32[256,256]{0,1:T(8,128)} %copy.18, pred[]{:T(512)S(6)} %eq.23, f32[2,256,256]{2,1,0:T(8,128)} %copy-done.6), kind=kOutput, calls=%fused_computation.21 | convolution fusion | flops 50413568 | bytes 786433 | tf_op jit(solution)/shard_map/dot_general | solution.py:45
  93.6 1.4 fusion.33
  95.1 1.4 convolution_add_fusion.2
  96.9 1.3 convolution_add_fusion.3
  99.6 1.2 fusion.15
  101.5 0.7 convolution_bitcast_fusion
  103.3 1.5 %multiply_reduce_fusion.1 = (f32[64]{0:T(128)S(1)}, f32[64]{0:T(128)S(1)}, f32[64]{0:T(128)S(1)}, f32[64]{0:T(128)S(1)}, f32[4096,64]{0,1:T(8,128)}) fusion(f32[4096,64]{0,1:T(8,128)S(1)} %copy-done.8, f32[4096,64]{0,1:T(8,128)S(1)} %copy-done.3, f32[4096,64]{0,1:T(8,128)S(1)} %bitcast.152, f32[1024,64]{0,1:T(8,128)S(1)} %copy-done.15, ...), kind=kLoop, calls=%fused_computation.35 | loop fusion | flops 3669760 | bytes 5243904 | tf_op jit(solution)/shard_map/reduce_sum | solution.py:120
  104.8 37.6 %all-reduce = (f32[64]{0:T(128)S(1)}, f32[64]{0:T(128)S(1)}, f32[64]{0:T(128)S(1)}, f32[64]{0:T(128)S(1)}) all-reduce(f32[64]{0:T(128)S(1)} %get-tuple-element.6, f32[64]{0:T(128)S(1)} %get-tuple-element.5, f32[64]{0:T(128)S(1)} %get-tuple-element.4, f32[64]{0:T(128)S(1)} %get-tuple-element.3), channel_id=1, replica_groups=mesh['grp'=4,'leaf'=8] {'grp','leaf'}, use_global_device_ids=true, to_apply=%region_1.2 | all-reduce | flops 256 | bytes 2048 | tf_op jit(solution)/shard_map/psum | solution.py:116
  142.4 3.8 %multiply_add_fusion = (f32[4096,64]{0,1:T(8,128)}, f32[4096,64]{0,1:T(8,128)}, f32[4096,64]{0,1:T(8,128)}) fusion(f32[4096,64]{0,1:T(8,128)S(1)} %copy-done.3, f32[64]{0:T(128)S(1)} %get-tuple-element.21, f32[4096,64]{0,1:T(8,128)} %param.13, f32[4096,64]{0,1:T(8,128)} %get-tuple-element.23, f32[64]{0:T(128)S(1)} %get-tuple-element.22, f32[4096,64]{0,1:T(8,128)} %param.12), kind=kLoop, calls=%fused_computation.33 | loop fusion | flops 1572864 | bytes 7340544 | tf_op jit(solution)/shard_map/add | solution.py:129
  (73 shorter events, 10.2 us)
Async XLA Ops:
  0.6 1.9 %copy-start = (bf16[4,1024,256]{2,1,0:T(8,128)(2,1)S(1)}, bf16[4,1024,256]{2,1,0:T(8,128)(2,1)}, u32[]{:S(2)}) copy-start(bf16[4,1024,256]{2,1,0:T(8,128)(2,1)} %param.16) | copy-start | bytes 6291460
  0.6 2.4 %copy-start.9 = (bf16[4,256,256]{2,1,0:T(8,128)(2,1)S(1)}, bf16[4,256,256]{2,1,0:T(8,128)(2,1)}, u32[]{:S(2)}) copy-start(bf16[4,256,256]{2,1,0:T(8,128)(2,1)} %param.17) | copy-start | bytes 1572868
  2.1 4.9 %copy-start.1 = (bf16[4096,64]{0,1:T(8,128)(2,1)S(1)}, bf16[4096,64]{0,1:T(8,128)(2,1)}, u32[]{:S(2)}) copy-start(bf16[4096,64]{0,1:T(8,128)(2,1)} %param.11) | copy-start | bytes 1572868
  4.0 37.9 %collective-permute-start.2 = (f32[256,64]{0,1:T(8,128)}, f32[256,64]{0,1:T(8,128)}, u32[]{:S(2)}, u32[]{:S(2)}) collective-permute-start(f32[256,64]{0,1:T(8,128)} %bitcast.13), channel_id=1, source_target_pairs={{0,1},{1,0},{2,3},{3,2},{4,5},{5,4},{6,7},{7,6},{8,9},{9,8},{10,11... | collective-permute-start | bytes 196616 | tf_op jit(solution)/shard_map/ppermute | solution.py:28
  7.8 57.3 %collective-permute-start = (bf16[1024,128]{0,1:T(8,128)(2,1)}, bf16[1024,128]{0,1:T(8,128)(2,1)}, u32[]{:S(2)}, u32[]{:S(2)}) collective-permute-start(bf16[1024,128]{0,1:T(8,128)(2,1)} %get-tuple-element.26), channel_id=1, source_target_pairs={{0,1},{1,2},{2,3},{3,4},{4,5},{5,6},{6,7},{7,8},{8,9},{9,10},{10,1... | collective-permute-start | bytes 786440 | tf_op jit(solution)/shard_map/ppermute | solution.py:18
  10.4 54.6 %collective-permute-start.1 = (bf16[1024,128]{0,1:T(8,128)(2,1)}, bf16[1024,128]{0,1:T(8,128)(2,1)}, u32[]{:S(2)}, u32[]{:S(2)}) collective-permute-start(bf16[1024,128]{0,1:T(8,128)(2,1)} %get-tuple-element.25), channel_id=1, source_target_pairs={{1,0},{2,1},{3,2},{4,3},{5,4},{6,5},{7,6},{8,7},{9,8},{10,9},{11,1... | collective-permute-start | bytes 786440 | tf_op jit(solution)/shard_map/ppermute | solution.py:20
  12.5 4.6 %copy-start.12 = (bf16[2,256,256]{2,1,0:T(8,128)(2,1)S(1)}, bf16[2,256,256]{2,1,0:T(8,128)(2,1)}, u32[]{:S(2)}) copy-start(bf16[2,256,256]{2,1,0:T(8,128)(2,1)} %param.21) | copy-start | bytes 786436
  17.1 0.8 copy-start.6
  21.2 6.5 %copy-start.22 = (s32[4,3]{1,0:T(4,128)S(1)}, s32[4,3]{1,0:T(4,128)}, u32[]{:S(2)}) copy-start(s32[4,3]{1,0:T(4,128)} %param.15) | copy-start | bytes 148
  22.3 0.9 copy-start.4
  41.9 16.7 %copy-start.7 = (f32[2,2,256,256]{3,2,1,0:T(8,128)S(1)}, f32[2,2,256,256]{3,2,1,0:T(8,128)}, u32[]{:S(2)}) copy-start(f32[2,2,256,256]{3,2,1,0:T(8,128)} %convert_element_type.74) | copy-start | bytes 3145732
  43.3 6.9 %collective-permute-start.3 = (f32[256,64]{0,1:T(8,128)S(1)}, f32[256,64]{0,1:T(8,128)S(1)}, u32[]{:S(2)}, u32[]{:S(2)}) collective-permute-start(f32[256,64]{0,1:T(8,128)S(1)} %convolution_add_fusion.8), channel_id=1, source_target_pairs={{0,2},{1,3},{2,0},{3,1},{4,6},{5,7},{6,4},{7,5},{8,10},{9,11},{10,... | collective-permute-start | bytes 196616 | tf_op jit(solution)/shard_map/ppermute | solution.py:28
  50.2 8.3 %copy-start.17 = (f32[256,64]{0,1:T(8,128)}, f32[256,64]{0,1:T(8,128)S(1)}, u32[]{:S(2)}) copy-start(f32[256,64]{0,1:T(8,128)S(1)} %collective-permute-done.3) | copy-start | bytes 196612
  51.5 5.6 %collective-permute-start.4 = (f32[256,64]{0,1:T(8,128)S(1)}, f32[256,64]{0,1:T(8,128)S(1)}, u32[]{:S(2)}, u32[]{:S(2)}) collective-permute-start(f32[256,64]{0,1:T(8,128)S(1)} %convolution_add_fusion.7), channel_id=1, source_target_pairs={{0,4},{1,5},{2,6},{3,7},{4,0},{5,1},{6,2},{7,3},{8,12},{9,13},{10,... | collective-permute-start | bytes 196616 | tf_op jit(solution)/shard_map/ppermute | solution.py:28
  57.1 1.4 copy-start.19
  58.5 1.3 collective-permute-start.5
  59.8 1.2 copy-start.21
  61.1 31.0 %collective-permute-start.6 = (f32[256,64]{1,0:T(8,128)}, f32[256,64]{1,0:T(8,128)}, u32[]{:S(2)}, u32[]{:S(2)}) collective-permute-start(f32[256,64]{1,0:T(8,128)} %convolution_add_fusion.1), channel_id=1, source_target_pairs={{0,16},{8,24},{16,0},{24,8},{1,17},{9,25},{17,1},{25,9},{2,18},{10... | collective-permute-start | bytes 196616 | tf_op jit(solution)/shard_map/ppermute | solution.py:28
  67.0 6.0 %copy-start.24 = (f32[1024]{0:T(1024)S(1)}, f32[1024]{0:T(1024)}, u32[]{:S(2)}) copy-start(f32[1024]{0:T(1024)} %get-tuple-element.9) | copy-start | bytes 12292
  79.6 6.4 %copy-start.23 = (f32[1024]{0:T(1024)S(1)}, f32[1024]{0:T(1024)}, u32[]{:S(2)}) copy-start(f32[1024]{0:T(1024)} %get-tuple-element.10) | copy-start | bytes 12292
  92.0 4.4 %copy-start.2 = (f32[3,2,256,256]{3,2,1,0:T(8,128)S(1)}, f32[3,2,256,256]{3,2,1,0:T(8,128)}, u32[]{:S(2)}) copy-start(f32[3,2,256,256]{3,2,1,0:T(8,128)} %convert_element_type.72) | copy-start | bytes 4718596
  92.0 4.9 %copy-start.5 = (f32[3,256,256]{2,1,0:T(8,128)S(1)}, f32[3,256,256]{2,1,0:T(8,128)}, u32[]{:S(2)}) copy-start(f32[3,256,256]{2,1,0:T(8,128)} %copy-done.4) | copy-start | bytes 2359300
  92.0 4.9 %copy-start.20 = (f32[256,64]{0,1:T(8,128)S(1)}, f32[256,64]{0,1:T(8,128)}, u32[]{:S(2)}) copy-start(f32[256,64]{0,1:T(8,128)} %copy-done.19) | copy-start | bytes 196612
  92.0 6.6 %copy-start.11 = (f32[256,256]{0,1:T(8,128)S(1)}, f32[256,256]{0,1:T(8,128)}, u32[]{:S(2)}) copy-start(f32[256,256]{0,1:T(8,128)} %copy.15) | copy-start | bytes 786436
  92.0 6.6 %copy-start.18 = (f32[256,64]{0,1:T(8,128)S(1)}, f32[256,64]{0,1:T(8,128)}, u32[]{:S(2)}) copy-start(f32[256,64]{0,1:T(8,128)} %copy-done.17) | copy-start | bytes 196612
  96.5 4.3 %copy-start.10 = (bf16[4,256,256]{2,1,0:T(8,128)(2,1)S(1)}, bf16[4,256,256]{2,1,0:T(8,128)(2,1)}, u32[]{:S(2)}) copy-start(bf16[4,256,256]{2,1,0:T(8,128)(2,1)} %param.17) | copy-start | bytes 1572868
  101.5 1.2 copy-start.3
  101.5 1.5 %copy-start.8 = (f32[4096,64]{0,1:T(8,128)S(1)}, f32[4096,64]{0,1:T(8,128)}, u32[]{:S(2)}) copy-start(f32[4096,64]{0,1:T(8,128)} %param.13) | copy-start | bytes 3145732
  101.5 1.6 %copy-start.13 = (f32[1024,64]{0,1:T(8,128)S(1)}, f32[1024,64]{0,1:T(8,128)}, u32[]{:S(2)}) copy-start(f32[1024,64]{0,1:T(8,128)} %fusion.10) | copy-start | bytes 786436
  101.5 1.6 %copy-start.14 = (f32[1024,64]{0,1:T(8,128)S(1)}, f32[1024,64]{0,1:T(8,128)}, u32[]{:S(2)}) copy-start(f32[1024,64]{0,1:T(8,128)} %fusion.12) | copy-start | bytes 786436
  101.5 1.7 %copy-start.15 = (f32[1024,64]{0,1:T(8,128)S(1)}, f32[1024,64]{0,1:T(8,128)}, u32[]{:S(2)}) copy-start(f32[1024,64]{0,1:T(8,128)} %fusion.13) | copy-start | bytes 786436
  101.5 1.8 %copy-start.16 = (f32[1024,64]{0,1:T(8,128)S(1)}, f32[1024,64]{0,1:T(8,128)}, u32[]{:S(2)}) copy-start(f32[1024,64]{0,1:T(8,128)} %fusion.11) | copy-start | bytes 786436
where the time goes:
time: 147 us; the launch traced here: 146 us
  matrix products  48.3 us (33%)
  blocking collectives  37.6 us (26%)
  starting transfers between devices  18.4 us (13%)
  other arithmetic  17.2 us (12%)
  local copies, waits for them, and re-layouts  15.7 us (11%)
  between operations  5.92 us (4%)
  waiting for transfers between devices  3.06 us (2%)
    psum x1, blocking collectives, body(): lax.psum((jnp.sum(residual * residual, axis=0), jnp.sum(direction * image...  37.6 us
    dot_general x4, matrix products, body(): jnp.dot(kern, window[:, dim:], preferred_element_type=jnp.float32)  25 us
    ppermute x5, starting transfers between devices, swapped(): lax.ppermute(value, axis, [(i, i ^ 1 << stride) for i in range(lax.axis_s...  14.5 us
    dot_general x5, matrix products, couple(): return (q_mine, jnp.dot(coupling_mat, other, precision=highest))  6.09 us
    dot_general x4, matrix products, join_pair(): jnp.dot(q_other.T, other, precision=highest)  5.34 us
    dot_general x4, matrix products, join_pair(): jnp.dot(q_mine.T, own, precision=highest)  5.18 us
    squeeze x4, local copies, waits for them, and re-layouts, body(): records.append(couple(other, side, inner_q[level], inner_b[level]))  4.55 us
    dot_general x5, matrix products, body(): incoming = mine + jnp.dot(q_mine, incoming, precision=highest)  3.93 us
  transfers between devices with their start and end apart: 7, of which 3 were waited for; matrix products, arithmetic and copies ran while one was open for 41% of the time, Pallas kernels for 0%

commit v1 on v0

--- a/solution.py
+++ b/solution.py
@@ -114,13 +114,16 @@
     ).reshape(-1, nrhs)
     image = ridge * direction + near_term + far_term
     rr, pq, rq, qq = lax.psum(
-        (
-            jnp.sum(residual * residual, axis=0),
-            jnp.sum(direction * image, axis=0),
-            jnp.sum(residual * image, axis=0),
-            jnp.sum(image * image, axis=0),
+        lax.psum(
+            (
+                jnp.sum(residual * residual, axis=0),
+                jnp.sum(direction * image, axis=0),
+                jnp.sum(residual * image, axis=0),
+                jnp.sum(image * image, axis=0),
+            ),
+            "leaf",
         ),
-        ("grp", "leaf"),
+        "grp",
     )
     alpha = rr / pq
     new_solution = solution + alpha * direction

time: 147 us -> 134 us (0.912)
  blocking collectives: 37.6 us -> 23.8 us
    psum x1, blocking collectives: 37.6 us -> 17.9 us  [body(): lax.psum((jnp.sum(residual * residual, axis=0), jnp.sum(direction * image...]
    psum x0 -> x1, blocking collectives: none -> 5.86 us  [body(): lax.psum(lax.psum((jnp.sum(residual * residual, axis=0), jnp.sum(directio...]
  transfers between devices with their start and end apart: 7 -> 7, of which waited for: 3 -> 3; matrix products, arithmetic and copies ran while one was open for 41% -> 45% of each run, Pallas kernels for 0% -> 0%
where the time goes in v1:
time: 134 us; the launch traced here: 133 us
  matrix products  48.3 us (36%)
  blocking collectives  23.8 us (18%)
  starting transfers between devices  18.4 us (14%)
  other arithmetic  17.2 us (13%)
  local copies, waits for them, and re-layouts  15.8 us (12%)
  between operations  6.11 us (5%)
  waiting for transfers between devices  3.06 us (2%)
    dot_general x4, matrix products, body(): jnp.dot(kern, window[:, dim:], preferred_element_type=jnp.float32)  25 us
    psum x1, blocking collectives, body(): lax.psum((jnp.sum(residual * residual, axis=0), jnp.sum(direction * image...  17.9 us
    ppermute x5, starting transfers between devices, swapped(): lax.ppermute(value, axis, [(i, i ^ 1 << stride) for i in range(lax.axis_s...  14.5 us
    dot_general x5, matrix products, couple(): return (q_mine, jnp.dot(coupling_mat, other, precision=highest))  6.09 us
    psum x1, blocking collectives, body(): lax.psum(lax.psum((jnp.sum(residual * residual, axis=0), jnp.sum(directio...  5.86 us
    dot_general x4, matrix products, join_pair(): jnp.dot(q_other.T, other, precision=highest)  5.35 us
    dot_general x4, matrix products, join_pair(): jnp.dot(q_mine.T, own, precision=highest)  5.17 us
    squeeze x4, local copies, waits for them, and re-layouts, body(): records.append(couple(other, side, inner_q[level], inner_b[level]))  4.58 us
  transfers between devices with their start and end apart: 7, of which 3 were waited for; matrix products, arithmetic and copies ran while one was open for 45% of the time, Pallas kernels for 0%

profile of v1, /device:TPU:0, one launch (start us, length us, event | category | flops | bytes accessed | tf_op | source)
XLA Modules:
  0.0 132.7 jit_solution(14895118023645145456)
XLA Ops:
  0.7 1.4 %convert_element_type.59 = bf16[4096,64]{0,1:T(8,128)(2,1)S(1)} convert(f32[4096,64]{0,1:T(8,128)} %param.14) | non-fusion elementwise | flops 262144 | bytes 1572864 | tf_op jit(solution)/shard_map/convert_element_type | solution.py:76
  3.0 1.0 fusion.103
  4.0 3.0 %collective-permute-start.2 = (f32[256,64]{0,1:T(8,128)}, f32[256,64]{0,1:T(8,128)}, u32[]{:S(2)}, u32[]{:S(2)}) collective-permute-start(f32[256,64]{0,1:T(8,128)} %bitcast.13), channel_id=1, source_target_pairs={{0,1},{1,0},{2,3},{3,2},{4,5},{5,4},{6,7},{7,6},{8,9},{9,8},{10,11... | collective-permute-start | bytes 196616 | tf_op jit(solution)/shard_map/ppermute | solution.py:28
  7.0 0.8 pad_maximum_fusion.14
  7.8 2.6 %collective-permute-start = (bf16[1024,128]{0,1:T(8,128)(2,1)}, bf16[1024,128]{0,1:T(8,128)(2,1)}, u32[]{:S(2)}, u32[]{:S(2)}) collective-permute-start(bf16[1024,128]{0,1:T(8,128)(2,1)} %get-tuple-element.30), channel_id=1, source_target_pairs={{0,1},{1,2},{2,3},{3,4},{4,5},{5,6},{6,7},{7,8},{8,9},{9,10},{10,1... | collective-permute-start | bytes 786440 | tf_op jit(solution)/shard_map/ppermute | solution.py:18
  10.4 1.3 collective-permute-start.1
  11.7 0.7 multiply_reduce_fusion.11
  12.5 2.5 %convert_element_type.72 = f32[3,2,256,256]{3,2,1,0:T(8,128)} convert(bf16[3,2,256,256]{3,2,1,0:T(8,128)(2,1)} %param.18) | non-fusion elementwise | flops 393216 | bytes 2359296 | tf_op jit(solution)/shard_map/convert_element_type | solution.py:83
  14.9 2.1 %convert_element_type.74 = f32[2,2,256,256]{3,2,1,0:T(8,128)} convert(bf16[2,2,256,256]{3,2,1,0:T(8,128)(2,1)} %param.20) | non-fusion elementwise | flops 262144 | bytes 1572864 | tf_op jit(solution)/shard_map/convert_element_type | solution.py:85
  17.1 0.8 copy-done.6
  17.9 0.7 slice_bitcast_fusion.1
  18.6 1.8 %copy.18 = f32[256,256]{0,1:T(8,128)} copy(f32[256,256]{1,0:T(8,128)} %get-tuple-element.35) | data formatting | bytes 524288 | tf_op jit(solution)/shard_map/squeeze | solution.py:96
  20.4 0.8 copy.17
  21.2 1.1 convert_element_type.71
  22.3 0.9 copy-done.4
  23.2 0.9 slice_bitcast_fusion.4
  24.1 1.8 %copy.16 = f32[256,256]{0,1:T(8,128)} copy(f32[256,256]{1,0:T(8,128)} %get-tuple-element.32) | data formatting | bytes 524288 | tf_op jit(solution)/shard_map/squeeze | solution.py:91
  25.9 0.9 copy.15
  26.7 1.1 copy.14
  34.9 1.9 %fusion.50 = f32[256,64]{0,1:T(8,128)} fusion(f32[3,2,256,256]{3,2,1,0:T(8,128)} %convert_element_type.72, pred[]{:T(512)S(6)} %eq.19, f32[64,256,1]{1,0,2:T(8,128)} %fusion.103), kind=kOutput, calls=%fused_computation.92 | convolution fusion | flops 50397184 | bytes 655361 | tf_op jit(solution)/shard_map/dot_general | solution.py:52
  36.8 1.4 %fusion.29 = f32[256,64]{1,0:T(8,128)S(1)} fusion(f32[2,2,256,256]{3,2,1,0:T(8,128)} %convert_element_type.74, pred[]{:T(512)S(6)} %eq.23), kind=kOutput, calls=%fused_computation.61 | convolution fusion | flops 50397184 | bytes 589825 | tf_op jit(solution)/shard_map/dot_general | solution.py:110
  40.8 0.7 broadcast_in_dim.12
  42.2 1.4 %convolution_add_fusion.8 = f32[256,64]{0,1:T(8,128)S(1)} fusion(f32[256,64]{0,1:T(8,128)} %fusion.50, f32[256,64]{0,1:T(8,128)} %collective-permute-done.2, f32[3,2,256,256]{3,2,1,0:T(8,128)} %convert_element_type.72, pred[]{:T(512)S(6)} %eq.19), kind=kOutput, calls=%fused_computation.30 | convolution fusion | flops 50413568 | bytes 720897 | tf_op jit(solution)/shard_map/dot_general | solution.py:52
  43.6 4.5 %collective-permute-start.3 = (f32[256,64]{0,1:T(8,128)S(1)}, f32[256,64]{0,1:T(8,128)S(1)}, u32[]{:S(2)}, u32[]{:S(2)}) collective-permute-start(f32[256,64]{0,1:T(8,128)S(1)} %convolution_add_fusion.8), channel_id=1, source_target_pairs={{0,2},{1,3},{2,0},{3,1},{4,6},{5,7},{6,4},{7,5},{8,10},{9,11},{10,... | collective-permute-start | bytes 196616 | tf_op jit(solution)/shard_map/ppermute | solution.py:28
  48.1 1.3 fusion.45
  49.4 1.1 collective-permute-done.3
  50.5 1.3 %convolution_add_fusion.7 = f32[256,64]{0,1:T(8,128)S(1)} fusion(f32[256,64]{0,1:T(8,128)S(1)} %fusion.45, f32[256,64]{0,1:T(8,128)S(1)} %collective-permute-done.3, f32[3,2,256,256]{3,2,1,0:T(8,128)} %convert_element_type.72, pred[]{:T(512)S(6)} %eq.20), kind=kOutput, calls=%fused_computation.29 | convolution fusion | flops 50413568 | bytes 720897 | tf_op jit(solution)/shard_map/dot_general | solution.py:52
  51.8 2.9 %collective-permute-start.4 = (f32[256,64]{0,1:T(8,128)S(1)}, f32[256,64]{0,1:T(8,128)S(1)}, u32[]{:S(2)}, u32[]{:S(2)}) collective-permute-start(f32[256,64]{0,1:T(8,128)S(1)} %convolution_add_fusion.7), channel_id=1, source_target_pairs={{0,4},{1,5},{2,6},{3,7},{4,0},{5,1},{6,2},{7,3},{8,12},{9,13},{10,... | collective-permute-start | bytes 196616 | tf_op jit(solution)/shard_map/ppermute | solution.py:28
  54.8 1.3 fusion.40
  56.1 1.3 %collective-permute-done.4 = f32[256,64]{0,1:T(8,128)S(1)} collective-permute-done((f32[256,64]{0,1:T(8,128)S(1)}, f32[256,64]{0,1:T(8,128)S(1)}, u32[]{:S(2)}, u32[]{:S(2)}) %collective-permute-start.4) | collective-permute-done | bytes 65568 | tf_op jit(solution)/shard_map/ppermute | solution.py:28
  57.4 1.3 %convolution_add_fusion.6 = f32[256,64]{0,1:T(8,128)S(1)} fusion(f32[256,64]{0,1:T(8,128)S(1)} %fusion.40, f32[256,64]{0,1:T(8,128)S(1)} %collective-permute-done.4, f32[3,2,256,256]{3,2,1,0:T(8,128)} %convert_element_type.72, pred[]{:T(512)S(6)} %eq.21), kind=kOutput, calls=%fused_computation.28 | convolution fusion | flops 50413568 | bytes 720897 | tf_op jit(solution)/shard_map/dot_general | solution.py:52
  60.1 1.2 convolution_add_fusion.1
  61.4 4.0 %collective-permute-start.6 = (f32[256,64]{1,0:T(8,128)}, f32[256,64]{1,0:T(8,128)}, u32[]{:S(2)}, u32[]{:S(2)}) collective-permute-start(f32[256,64]{1,0:T(8,128)} %convolution_add_fusion.1), channel_id=1, source_target_pairs={{0,16},{8,24},{16,0},{24,8},{1,17},{9,25},{17,1},{25,9},{2,18},{10... | collective-permute-start | bytes 196616 | tf_op jit(solution)/shard_map/ppermute | solution.py:28
  65.4 2.0 %multiply_reduce_fusion.7 = (f32[3072]{0:T(1024)}, f32[3072]{0:T(1024)}, f32[3072]{0:T(1024)}, f32[3072]{0:T(1024)S(1)}) fusion(bf16[4096,64]{0,1:T(8,128)(2,1)S(1)} %convert_element_type.59, bf16[4096,64]{0,1:T(8,128)(2,1)S(1)} %copy-done.1, bf16[1024,128]{0,1:T(8,128)(2,1)} %collective-permute-done, bf16[1024,128]{0,1:T(8,128)(2,1)} %collective-permute-done.1), kind=kLoop, calls=%fused_computation.43 | loop fusion | flops 4313088 | bytes 2408448 | tf_op jit(solution)/shard_map/reduce_sum | solution.py:35
  67.3 6.0 %fusion.10 = f32[1024,64]{0,1:T(8,128)} fusion(f32[3072]{0:T(1024)} %mul.164, f32[3072]{0:T(1024)} %get-tuple-element.13, f32[1024]{0:T(1024)} %get-tuple-element.11, bf16[4096,64]{0,1:T(8,128)(2,1)S(1)} %convert_element_type.59, bf16[4096,64]{0,1:T(8,128)(2,1)S(1)} %copy-done.1), kind=kOutput, calls=%fused_computation.14 | convolution fusion | flops 827326464 | bytes 1208320 | tf_op jit(solution)/shard_map/dot_general | solution.py:106
  73.3 6.6 %fusion.12 = f32[1024,64]{0,1:T(8,128)} fusion(f32[3072]{0:T(1024)} %mul.157, f32[3072]{0:T(1024)} %get-tuple-element.7, f32[1024]{0:T(1024)S(1)} %copy-done.24, bf16[1024,128]{0,1:T(8,128)(2,1)} %collective-permute-done, bf16[4096,64]{0,1:T(8,128)(2,1)S(1)} %convert_element_type.59, bf16[4096,64]{0,1:T(8,128)(2,1)S(1)} %copy-done.1), kind=kOutput, calls=%fused_computation.16 | convolution fusion | flops 829685760 | bytes 3043328 | tf_op jit(solution)/shard_map/dot_general | solution.py:106
  79.9 6.4 %fusion.13 = f32[1024,64]{0,1:T(8,128)} fusion(f32[3072]{0:T(1024)} %mul.179, f32[3072]{0:T(1024)} %get-tuple-element.8, f32[1024]{0:T(1024)} %get-tuple-element.12, bf16[1024,128]{0,1:T(8,128)(2,1)} %collective-permute-done.1, bf16[4096,64]{0,1:T(8,128)(2,1)S(1)} %convert_element_type.59, bf16[4096,64]{0,1:T(8,128)(2,1)S(1)} %copy-done.1), kind=kOutput, calls=%fused_computation.17 | convolution fusion | flops 829685760 | bytes 3043328 | tf_op jit(solution)/shard_map/dot_general | solution.py:106
  86.3 6.0 %fusion.11 = f32[1024,64]{0,1:T(8,128)} fusion(f32[3072]{0:T(1024)} %mul.171, f32[3072]{0:T(1024)S(1)} %get-tuple-element.14, f32[1024]{0:T(1024)S(1)} %copy-done.23, bf16[4096,64]{0,1:T(8,128)(2,1)S(1)} %convert_element_type.59, bf16[4096,64]{0,1:T(8,128)(2,1)S(1)} %copy-done.1), kind=kOutput, calls=%fused_computation.15 | convolution fusion | flops 827326464 | bytes 1208320 | tf_op jit(solution)/shard_map/dot_general | solution.py:106
  92.3 1.6 %convolution_add_fusion = f32[256,64]{1,0:T(8,128)S(1)} fusion(f32[256,64]{1,0:T(8,128)S(1)} %fusion.29, f32[256,64]{1,0:T(8,128)} %collective-permute-done.6, f32[256,256]{0,1:T(8,128)} %copy.18, pred[]{:T(512)S(6)} %eq.23, f32[2,256,256]{2,1,0:T(8,128)} %copy-done.6), kind=kOutput, calls=%fused_computation.21 | convolution fusion | flops 50413568 | bytes 786433 | tf_op jit(solution)/shard_map/dot_general | solution.py:45
  93.9 1.4 %fusion.33 = f32[256,64]{1,0:T(8,128)S(1)} fusion(f32[256,64]{1,0:T(8,128)S(1)} %convolution_add_fusion, f32[2,2,256,256]{3,2,1,0:T(8,128)} %convert_element_type.74, pred[]{:T(512)S(6)} %eq.22), kind=kOutput, calls=%fused_computation.72 | convolution fusion | flops 50397184 | bytes 655361 | tf_op jit(solution)/shard_map/dot_general | solution.py:110
  95.3 1.4 %convolution_add_fusion.2 = f32[256,64]{1,0:T(8,128)S(1)} fusion(f32[256,64]{1,0:T(8,128)S(1)} %fusion.33, f32[256,64]{0,1:T(8,128)} %copy-done.21, f32[256,256]{0,1:T(8,128)} %copy.17, pred[]{:T(512)S(6)} %eq.22, f32[2,256,256]{2,1,0:T(8,128)} %copy-done.6), kind=kOutput, calls=%fused_computation.23 | convolution fusion | flops 50413568 | bytes 720897 | tf_op jit(solution)/shard_map/dot_general | solution.py:45
  97.2 1.3 convolution_add_fusion.3
  99.9 1.2 fusion.15
  101.8 0.7 convolution_bitcast_fusion
  103.6 1.5 %multiply_reduce_fusion.1 = (f32[64]{0:T(128)S(1)}, f32[64]{0:T(128)S(1)}, f32[64]{0:T(128)S(1)}, f32[64]{0:T(128)S(1)}, f32[4096,64]{0,1:T(8,128)}) fusion(f32[4096,64]{0,1:T(8,128)S(1)} %copy-done.8, f32[4096,64]{0,1:T(8,128)S(1)} %copy-done.3, f32[4096,64]{0,1:T(8,128)S(1)} %bitcast.152, f32[1024,64]{0,1:T(8,128)S(1)} %copy-done.15, ...), kind=kLoop, calls=%fused_computation.35 | loop fusion | flops 3669760 | bytes 5243904 | tf_op jit(solution)/shard_map/reduce_sum | solution.py:121
  105.1 17.9 %all-reduce = (f32[64]{0:T(128)S(1)}, f32[64]{0:T(128)S(1)}, f32[64]{0:T(128)S(1)}, f32[64]{0:T(128)S(1)}) all-reduce(f32[64]{0:T(128)S(1)} %get-tuple-element.6, f32[64]{0:T(128)S(1)} %get-tuple-element.5, f32[64]{0:T(128)S(1)} %get-tuple-element.4, f32[64]{0:T(128)S(1)} %get-tuple-element.3), channel_id=1, replica_groups=mesh['grp'=4,'leaf'=8] {'leaf'}, use_global_device_ids=true, to_apply=%region_1.2 | all-reduce | flops 256 | bytes 2048 | tf_op jit(solution)/shard_map/psum | solution.py:117
  123.0 5.9 %all-reduce.1 = (f32[64]{0:T(128)S(1)}, f32[64]{0:T(128)S(1)}, f32[64]{0:T(128)S(1)}, f32[64]{0:T(128)S(1)}) all-reduce(f32[64]{0:T(128)S(1)} %get-tuple-element.15, f32[64]{0:T(128)S(1)} %get-tuple-element.16, f32[64]{0:T(128)S(1)} %get-tuple-element.17, f32[64]{0:T(128)S(1)} %get-tuple-element.18), channel_id=1, replica_groups=mesh['grp'=4,'leaf'=8] {'grp'}, use_global_device_ids=true, to_apply=%region_2.3 | all-reduce | flops 256 | bytes 2048 | tf_op jit(solution)/shard_map/psum | solution.py:116
  128.9 3.8 %multiply_add_fusion = (f32[4096,64]{0,1:T(8,128)}, f32[4096,64]{0,1:T(8,128)}, f32[4096,64]{0,1:T(8,128)}) fusion(f32[4096,64]{0,1:T(8,128)S(1)} %copy-done.3, f32[64]{0:T(128)S(1)} %get-tuple-element.25, f32[4096,64]{0,1:T(8,128)} %param.13, f32[4096,64]{0,1:T(8,128)} %get-tuple-element.27, f32[64]{0:T(128)S(1)} %get-tuple-element.26, f32[4096,64]{0,1:T(8,128)} %param.12), kind=kLoop, calls=%fused_computation.33 | loop fusion | flops 1572864 | bytes 7340544 | tf_op jit(solution)/shard_map/add | solution.py:132
  (74 shorter events, 10.9 us)
Async XLA Ops:
  0.6 1.9 %copy-start = (bf16[4,1024,256]{2,1,0:T(8,128)(2,1)S(1)}, bf16[4,1024,256]{2,1,0:T(8,128)(2,1)}, u32[]{:S(2)}) copy-start(bf16[4,1024,256]{2,1,0:T(8,128)(2,1)} %param.16) | copy-start | bytes 6291460
  0.6 2.4 %copy-start.9 = (bf16[4,256,256]{2,1,0:T(8,128)(2,1)S(1)}, bf16[4,256,256]{2,1,0:T(8,128)(2,1)}, u32[]{:S(2)}) copy-start(bf16[4,256,256]{2,1,0:T(8,128)(2,1)} %param.17) | copy-start | bytes 1572868
  2.1 4.9 %copy-start.1 = (bf16[4096,64]{0,1:T(8,128)(2,1)S(1)}, bf16[4096,64]{0,1:T(8,128)(2,1)}, u32[]{:S(2)}) copy-start(bf16[4096,64]{0,1:T(8,128)(2,1)} %param.11) | copy-start | bytes 1572868
  4.0 38.2 %collective-permute-start.2 = (f32[256,64]{0,1:T(8,128)}, f32[256,64]{0,1:T(8,128)}, u32[]{:S(2)}, u32[]{:S(2)}) collective-permute-start(f32[256,64]{0,1:T(8,128)} %bitcast.13), channel_id=1, source_target_pairs={{0,1},{1,0},{2,3},{3,2},{4,5},{5,4},{6,7},{7,6},{8,9},{9,8},{10,11... | collective-permute-start | bytes 196616 | tf_op jit(solution)/shard_map/ppermute | solution.py:28
  7.8 57.5 %collective-permute-start = (bf16[1024,128]{0,1:T(8,128)(2,1)}, bf16[1024,128]{0,1:T(8,128)(2,1)}, u32[]{:S(2)}, u32[]{:S(2)}) collective-permute-start(bf16[1024,128]{0,1:T(8,128)(2,1)} %get-tuple-element.30), channel_id=1, source_target_pairs={{0,1},{1,2},{2,3},{3,4},{4,5},{5,6},{6,7},{7,8},{8,9},{9,10},{10,1... | collective-permute-start | bytes 786440 | tf_op jit(solution)/shard_map/ppermute | solution.py:18
  10.4 54.9 %collective-permute-start.1 = (bf16[1024,128]{0,1:T(8,128)(2,1)}, bf16[1024,128]{0,1:T(8,128)(2,1)}, u32[]{:S(2)}, u32[]{:S(2)}) collective-permute-start(bf16[1024,128]{0,1:T(8,128)(2,1)} %get-tuple-element.29), channel_id=1, source_target_pairs={{1,0},{2,1},{3,2},{4,3},{5,4},{6,5},{7,6},{8,7},{9,8},{10,9},{11,1... | collective-permute-start | bytes 786440 | tf_op jit(solution)/shard_map/ppermute | solution.py:20
  12.5 4.6 %copy-start.12 = (bf16[2,256,256]{2,1,0:T(8,128)(2,1)S(1)}, bf16[2,256,256]{2,1,0:T(8,128)(2,1)}, u32[]{:S(2)}) copy-start(bf16[2,256,256]{2,1,0:T(8,128)(2,1)} %param.21) | copy-start | bytes 786436
  17.1 0.8 copy-start.6
  21.2 6.6 %copy-start.22 = (s32[4,3]{1,0:T(4,128)S(1)}, s32[4,3]{1,0:T(4,128)}, u32[]{:S(2)}) copy-start(s32[4,3]{1,0:T(4,128)} %param.15) | copy-start | bytes 148
  22.3 0.9 copy-start.4
  42.2 16.7 %copy-start.7 = (f32[2,2,256,256]{3,2,1,0:T(8,128)S(1)}, f32[2,2,256,256]{3,2,1,0:T(8,128)}, u32[]{:S(2)}) copy-start(f32[2,2,256,256]{3,2,1,0:T(8,128)} %convert_element_type.74) | copy-start | bytes 3145732
  43.6 6.9 %collective-permute-start.3 = (f32[256,64]{0,1:T(8,128)S(1)}, f32[256,64]{0,1:T(8,128)S(1)}, u32[]{:S(2)}, u32[]{:S(2)}) collective-permute-start(f32[256,64]{0,1:T(8,128)S(1)} %convolution_add_fusion.8), channel_id=1, source_target_pairs={{0,2},{1,3},{2,0},{3,1},{4,6},{5,7},{6,4},{7,5},{8,10},{9,11},{10,... | collective-permute-start | bytes 196616 | tf_op jit(solution)/shard_map/ppermute | solution.py:28
  50.5 8.3 %copy-start.17 = (f32[256,64]{0,1:T(8,128)}, f32[256,64]{0,1:T(8,128)S(1)}, u32[]{:S(2)}) copy-start(f32[256,64]{0,1:T(8,128)S(1)} %collective-permute-done.3) | copy-start | bytes 196612
  51.8 5.6 %collective-permute-start.4 = (f32[256,64]{0,1:T(8,128)S(1)}, f32[256,64]{0,1:T(8,128)S(1)}, u32[]{:S(2)}, u32[]{:S(2)}) collective-permute-start(f32[256,64]{0,1:T(8,128)S(1)} %convolution_add_fusion.7), channel_id=1, source_target_pairs={{0,4},{1,5},{2,6},{3,7},{4,0},{5,1},{6,2},{7,3},{8,12},{9,13},{10,... | collective-permute-start | bytes 196616 | tf_op jit(solution)/shard_map/ppermute | solution.py:28
  57.4 1.4 %copy-start.19 = (f32[256,64]{0,1:T(8,128)}, f32[256,64]{0,1:T(8,128)S(1)}, u32[]{:S(2)}) copy-start(f32[256,64]{0,1:T(8,128)S(1)} %collective-permute-done.4) | copy-start | bytes 196612
  58.8 1.3 collective-permute-start.5
  60.1 1.3 copy-start.21
  61.4 31.0 %collective-permute-start.6 = (f32[256,64]{1,0:T(8,128)}, f32[256,64]{1,0:T(8,128)}, u32[]{:S(2)}, u32[]{:S(2)}) collective-permute-start(f32[256,64]{1,0:T(8,128)} %convolution_add_fusion.1), channel_id=1, source_target_pairs={{0,16},{8,24},{16,0},{24,8},{1,17},{9,25},{17,1},{25,9},{2,18},{10... | collective-permute-start | bytes 196616 | tf_op jit(solution)/shard_map/ppermute | solution.py:28
  67.3 6.0 %copy-start.24 = (f32[1024]{0:T(1024)S(1)}, f32[1024]{0:T(1024)}, u32[]{:S(2)}) copy-start(f32[1024]{0:T(1024)} %get-tuple-element.9) | copy-start | bytes 12292
  79.9 6.4 %copy-start.23 = (f32[1024]{0:T(1024)S(1)}, f32[1024]{0:T(1024)}, u32[]{:S(2)}) copy-start(f32[1024]{0:T(1024)} %get-tuple-element.10) | copy-start | bytes 12292
  92.3 4.4 %copy-start.2 = (f32[3,2,256,256]{3,2,1,0:T(8,128)S(1)}, f32[3,2,256,256]{3,2,1,0:T(8,128)}, u32[]{:S(2)}) copy-start(f32[3,2,256,256]{3,2,1,0:T(8,128)} %convert_element_type.72) | copy-start | bytes 4718596
  92.3 4.9 %copy-start.5 = (f32[3,256,256]{2,1,0:T(8,128)S(1)}, f32[3,256,256]{2,1,0:T(8,128)}, u32[]{:S(2)}) copy-start(f32[3,256,256]{2,1,0:T(8,128)} %copy-done.4) | copy-start | bytes 2359300
  92.3 4.9 %copy-start.20 = (f32[256,64]{0,1:T(8,128)S(1)}, f32[256,64]{0,1:T(8,128)}, u32[]{:S(2)}) copy-start(f32[256,64]{0,1:T(8,128)} %copy-done.19) | copy-start | bytes 196612
  92.3 6.6 %copy-start.11 = (f32[256,256]{0,1:T(8,128)S(1)}, f32[256,256]{0,1:T(8,128)}, u32[]{:S(2)}) copy-start(f32[256,256]{0,1:T(8,128)} %copy.15) | copy-start | bytes 786436
  92.3 6.6 %copy-start.18 = (f32[256,64]{0,1:T(8,128)S(1)}, f32[256,64]{0,1:T(8,128)}, u32[]{:S(2)}) copy-start(f32[256,64]{0,1:T(8,128)} %copy-done.17) | copy-start | bytes 196612
  96.8 4.3 %copy-start.10 = (bf16[4,256,256]{2,1,0:T(8,128)(2,1)S(1)}, bf16[4,256,256]{2,1,0:T(8,128)(2,1)}, u32[]{:S(2)}) copy-start(bf16[4,256,256]{2,1,0:T(8,128)(2,1)} %param.17) | copy-start | bytes 1572868
  101.8 1.2 copy-start.3
  101.8 1.5 %copy-start.8 = (f32[4096,64]{0,1:T(8,128)S(1)}, f32[4096,64]{0,1:T(8,128)}, u32[]{:S(2)}) copy-start(f32[4096,64]{0,1:T(8,128)} %param.13) | copy-start | bytes 3145732
  101.8 1.6 %copy-start.13 = (f32[1024,64]{0,1:T(8,128)S(1)}, f32[1024,64]{0,1:T(8,128)}, u32[]{:S(2)}) copy-start(f32[1024,64]{0,1:T(8,128)} %fusion.10) | copy-start | bytes 786436
  101.8 1.6 %copy-start.14 = (f32[1024,64]{0,1:T(8,128)S(1)}, f32[1024,64]{0,1:T(8,128)}, u32[]{:S(2)}) copy-start(f32[1024,64]{0,1:T(8,128)} %fusion.12) | copy-start | bytes 786436
  101.8 1.7 %copy-start.15 = (f32[1024,64]{0,1:T(8,128)S(1)}, f32[1024,64]{0,1:T(8,128)}, u32[]{:S(2)}) copy-start(f32[1024,64]{0,1:T(8,128)} %fusion.13) | copy-start | bytes 786436
  101.8 1.8 %copy-start.16 = (f32[1024,64]{0,1:T(8,128)S(1)}, f32[1024,64]{0,1:T(8,128)}, u32[]{:S(2)}) copy-start(f32[1024,64]{0,1:T(8,128)} %fusion.11) | copy-start | bytes 786436
